TPU v7x, 32 devices: a whole 2x2x4 slice. The times are simulated.
32 devices in a mesh: seq: 16 (over z, x, core), fsdp: 2 (over y).
Axes of the slice: x: 2, y: 2, z: 4, core: 2. Of those that a mesh axis runs over, the one named last changes fastest.
Arguments:
- inputs: bfloat16 [2, 16384, 1024], P(None, 'seq', 'fsdp'), may hold values from -6 to 6
- first_factor: bfloat16 [128, 128, 128], P('seq'), may hold values from -0.5 to 0.5
- second_factor: bfloat16 [128, 128, 128], P('seq'), may hold values from -0.5 to 0.5
- gate_scale: float32 [1024], P('fsdp'), may hold values from -2 to 2
- gate_bias: float32 [1024], P('fsdp'), may hold values from -3 to 3
- in_weight: bfloat16 [1024, 4096], P('seq', 'fsdp'), may hold values from -0.1875 to 0.1875
- out_weight: bfloat16 [4096, 1024], P('fsdp', 'seq'), may hold values from -0.09375 to 0.09375
- cotangent: bfloat16 [2, 16384, 1024], P(None, 'seq', 'fsdp'), may hold values from -6 to 6
Outputs:
- result: bfloat16 [2, 16384, 1024], P(None, 'seq', 'fsdp')
- input_grad: bfloat16 [2, 16384, 1024], P(None, 'seq', 'fsdp')
- grad_in: float32 [1024, 4096], P('seq', 'fsdp')
- grad_out: float32 [4096, 1024], P('fsdp', 'seq')
All inputs are finite; a program needn't handle non-finite values.
Results may differ from a plain program's by a relative error of at most 0.0075.
Values may be sent and summed in bfloat16 or wider, within the bound.
A program may use at most 192 MiB of HBM per device.

v0:
```python
import jax
import jax.numpy as jnp
from jax import lax
from jax.sharding import PartitionSpec as P


def body(
    inputs, first_factor, second_factor, gate_scale, gate_bias, in_weight, out_weight, cotangent
):
    seq_count, tok_rows, chan_count = inputs.shape
    blocks = first_factor.shape[0]
    block_size = first_factor.shape[1]
    row_count = seq_count * tok_rows
    groups = lax.axis_size("fsdp")
    gate_gain = gate_scale.reshape(1, 1, 1, chan_count)
    gate_shift = gate_bias.reshape(1, 1, 1, chan_count)
    source = inputs.reshape(seq_count, blocks, block_size, chan_count)
    section_one = jnp.einsum(
        "mkn,smnc->smkc", first_factor, source, preferred_element_type=jnp.float32
    ).astype(jnp.bfloat16)
    turned, source_cols = (
        lax.all_to_all(section_one, "seq", split_axis=2, concat_axis=1, tiled=True),
        lax.all_to_all(source, "seq", split_axis=2, concat_axis=1, tiled=True),
    )
    section_two = jnp.einsum(
        "kjm,smkc->sjkc", second_factor, turned, preferred_element_type=jnp.float32
    ).astype(jnp.bfloat16)
    section_two = lax.optimization_barrier(section_two)
    gate_cols = jax.nn.sigmoid(gate_gain * source_cols.astype(jnp.float32) + gate_shift)
    gated_cols = (gate_cols * section_two.astype(jnp.float32)).astype(jnp.bfloat16)
    mixed_grid = lax.all_to_all(gated_cols, "seq", split_axis=1, concat_axis=2, tiled=True)
    mixed = mixed_grid.reshape(row_count, chan_count)
    full_in = lax.all_gather(in_weight, "seq", axis=0, tiled=True)
    full_out = lax.all_gather(out_weight, "seq", axis=1, tiled=True)
    mixed_all = lax.all_gather(mixed, "fsdp", axis=1, tiled=True)
    pre_act = jnp.dot(mixed_all, full_in, preferred_element_type=jnp.float32)
    hidden = jax.nn.silu(pre_act).astype(jnp.bfloat16)
    partial_out = jnp.dot(hidden, full_out, preferred_element_type=jnp.float32)
    received = lax.all_to_all(partial_out, "fsdp", split_axis=1, concat_axis=0, tiled=True)
    branch_sum = jnp.sum(received.reshape(groups, row_count, chan_count), axis=0)
    result = (
        (mixed.astype(jnp.float32) + branch_sum)
        .astype(jnp.bfloat16)
        .reshape(seq_count, tok_rows, chan_count)
    )
    upstream = cotangent.reshape(row_count, chan_count)
    upstream_all = lax.all_gather(upstream, "fsdp", axis=1, tiled=True)
    hidden_grad = lax.dot_general(
        upstream_all, full_out, (((1,), (1,)), ((), ())), preferred_element_type=jnp.float32
    )
    sigma = jax.nn.sigmoid(pre_act)
    pre_grad = (hidden_grad * sigma * (1.0 + pre_act * (1.0 - sigma))).astype(jnp.bfloat16)
    out_term = lax.dot_general(
        hidden, upstream_all, (((0,), (0,)), ((), ())), preferred_element_type=jnp.float32
    )
    grad_out = lax.psum_scatter(out_term, "seq", scatter_dimension=1, tiled=True) * (
        1.0 / block_size
    )
    in_term = lax.dot_general(
        mixed_all, pre_grad, (((0,), (0,)), ((), ())), preferred_element_type=jnp.float32
    )
    grad_in = lax.psum_scatter(in_term, "seq", scatter_dimension=0, tiled=True) * (1.0 / block_size)
    back_term = lax.dot_general(
        pre_grad, full_in, (((1,), (1,)), ((), ())), preferred_element_type=jnp.float32
    )
    back_pieces = lax.all_to_all(back_term, "fsdp", split_axis=1, concat_axis=0, tiled=True)
    back_sum = jnp.sum(back_pieces.reshape(groups, row_count, chan_count), axis=0)
    mixed_grad = (
        (upstream.astype(jnp.float32) + back_sum)
        .astype(jnp.bfloat16)
        .reshape(seq_count, blocks, block_size, chan_count)
    )
    grad_cols = lax.all_to_all(mixed_grad, "seq", split_axis=2, concat_axis=1, tiled=True).astype(
        jnp.float32
    )
    second_grad = (grad_cols * gate_cols).astype(jnp.bfloat16)
    gate_term = (
        grad_cols * section_two.astype(jnp.float32) * gate_cols * (1.0 - gate_cols) * gate_gain
    )
    gate_back = lax.all_to_all(
        gate_term.astype(jnp.bfloat16), "seq", split_axis=1, concat_axis=2, tiled=True
    ).astype(gate_term.dtype)
    first_grad = jnp.einsum(
        "kjm,sjkc->smkc", second_factor, second_grad, preferred_element_type=jnp.float32
    ).astype(jnp.bfloat16)
    first_rows = lax.all_to_all(first_grad, "seq", split_axis=1, concat_axis=2, tiled=True)
    input_sum = (
        jnp.einsum("mkn,smkc->smnc", first_factor, first_rows, preferred_element_type=jnp.float32)
        + gate_back
    )
    input_grad = input_sum.astype(jnp.bfloat16).reshape(seq_count, tok_rows, chan_count)
    return (result, input_grad, grad_in, grad_out)


def solution(mesh):
    in_specs = (
        P(None, "seq", "fsdp"),
        P("seq", None, None),
        P("seq", None, None),
        P("fsdp"),
        P("fsdp"),
        P("seq", "fsdp"),
        P("fsdp", "seq"),
        P(None, "seq", "fsdp"),
    )
    out_specs = (P(None, "seq", "fsdp"), P(None, "seq", "fsdp"), P("seq", "fsdp"), P("fsdp", "seq"))
    return jax.shard_map(body, mesh=mesh, in_specs=in_specs, out_specs=out_specs, check_vma=False)
```

profile of v0, /device:TPU:11, one launch (start us, length us, event | category | flops | bytes accessed | tf_op | source)
XLA Modules:
  0.0 827.8 jit_solution(12045572904759130662)
XLA Ops:
  11.4 6.6 all-to-all-start
  21.6 6.2 copy.84
  27.8 37.5 %all-to-all-done = bf16[2,8,128,512]{3,1,0,2:T(8,128)(2,1)S(1)} async-done(((bf16[2,8,128,512]{3,1,0,2:T(8,128)(2,1)}), bf16[2,8,128,512]{3,1,0,2:T(8,128)(2,1)S(1)}, u32[]{:S(2)}, u32[]{:S(2)}) %all-to-all-start) | async-done | bytes 2097184 | tf_op jit(solution)/shard_map/all_to_all | solution.py:23
  80.2 61.0 %all-to-all-done.1 = bf16[2,8,128,512]{3,0,1,2:T(2,128)(2,1)} async-done(((bf16[2,8,128,512]{3,0,1,2:T(2,128)(2,1)}), bf16[2,8,128,512]{3,0,1,2:T(2,128)(2,1)}, u32[]{:S(2)}, u32[]{:S(2)}) %all-to-all-start.1) | async-done | bytes 2097184 | tf_op jit(solution)/shard_map/all_to_all | solution.py:22
  154.6 52.1 %all_to_all.104 = bf16[2,128,8,512]{3,0,2,1:T(2,128)(2,1)S(1)} all-to-all(bf16[2,128,8,512]{3,0,2,1:T(2,128)(2,1)S(1)} %copy.88), channel_id=1, replica_groups=mesh['seq'=16,'fsdp'=2] {'seq'}, dimensions={1} | all-to-all | bytes 4194304 | tf_op jit(solution)/shard_map/all_to_all | solution.py:31
  211.5 54.9 %all-gather.5.cloned.1.call-done = bf16[2048,1024]{1,0:T(8,128)(2,1)} async-done(((bf16[2048,512]{1,0:T(8,128)(2,1)}), bf16[2048,1024]{1,0:T(8,128)(2,1)}) %all-gather.5.cloned.1.call-update) | async-done | bytes 4194320 | tf_op jit(solution)/shard_map/all_gather | solution.py:35
  266.4 18.6 %multiply_convert_fusion.1 = (bf16[2048,2048]{1,0:T(8,128)(2,1)}, f32[2048,2048]{1,0:T(8,128)}) fusion(bf16[2048,1024]{1,0:T(8,128)(2,1)} %all-gather.5.cloned.1.call-done, bf16[1024,2048]{1,0:T(8,128)(2,1)} %all-gather.7.cloned.1.call-done), kind=kOutput, calls=%fused_computation.1 | convolution fusion | flops 8610906112 | bytes 33554432 | tf_op jit(solution)/shard_map/dot_general | solution.py:36
  285.0 39.7 %all-gather.11.cloned.1.call-done = bf16[2048,1024]{1,0:T(8,128)(2,1)} async-done(((bf16[2048,512]{1,0:T(8,128)(2,1)}), bf16[2048,1024]{1,0:T(8,128)(2,1)}) %all-gather.11.cloned.1.call-update) | async-done | bytes 4194320 | tf_op jit(solution)/shard_map/all_gather | solution.py:47
  324.7 52.1 %all-gather.9.cloned.1.call-done = bf16[2048,1024]{0,1:T(8,128)(2,1)} async-done(((bf16[2048,64]{0,1:T(8,128)(2,1)}), bf16[2048,1024]{0,1:T(8,128)(2,1)}) %all-gather.9.cloned.1.call-update) | async-done | bytes 4194320 | tf_op jit(solution)/shard_map/all_gather | solution.py:34
  376.9 19.2 %multiply_convert_fusion = bf16[2048,2048]{1,0:T(8,128)(2,1)S(1)} fusion(f32[2048,2048]{1,0:T(8,128)} %get-tuple-element.5, bf16[2048,1024]{1,0:T(8,128)(2,1)} %all-gather.11.cloned.1.call-done, bf16[2048,1024]{0,1:T(8,128)(2,1)} %all-gather.9.cloned.1.call-done), kind=kOutput, calls=%fused_computation | convolution fusion | flops 8627683328 | bytes 33554432 | tf_op jit(solution)/shard_map/dot_general | solution.py:48
  399.3 11.4 %fusion.25 = f32[1024,2048]{1,0:T(8,128)} fusion(bf16[2048,1024]{1,0:T(8,128)(2,1)S(1)} %copy-done.13, bf16[2048,2048]{1,0:T(8,128)(2,1)S(1)} %multiply_convert_fusion), kind=kOutput, calls=%fused_computation.40 | convolution fusion | flops 8589934592 | bytes 20971520 | tf_op jit(solution)/shard_map/dot_general | solution.py:59
  410.8 12.6 %fusion.24 = f32[2048,1024]{0,1:T(8,128)S(1)} fusion(bf16[2048,2048]{1,0:T(8,128)(2,1)} %copy-done.14, bf16[1024,2048]{1,0:T(8,128)(2,1)} %all-gather.7.cloned.1.call-done), kind=kOutput, calls=%fused_computation.39 | convolution fusion | flops 8589934592 | bytes 20971520 | tf_op jit(solution)/shard_map/dot_general | solution.py:63
  423.3 96.6 %all_to_all.105 = f32[2048,2,512]{0,2,1:T(8,128)} all-to-all(f32[2048,2,512]{0,2,1:T(8,128)S(1)} %bitcast.96), channel_id=1, replica_groups=mesh['seq'=16,'fsdp'=2] {'fsdp'}, dimensions={1} | all-to-all | bytes 16777216 | tf_op jit(solution)/shard_map/all_to_all | solution.py:66
  519.9 6.6 reduce_sum.24
  526.5 5.5 copy.113
  537.5 6.2 all-to-all-start.5
  543.6 14.7 %fusion.23 = f32[2048,1024]{0,1:T(8,128)} fusion(bf16[2048,2048]{1,0:T(8,128)(2,1)} %get-tuple-element.4, bf16[2048,1024]{0,1:T(8,128)(2,1)} %all-gather.9.cloned.1.call-done), kind=kOutput, calls=%fused_computation.38 | convolution fusion | flops 8589934592 | bytes 20971520 | tf_op jit(solution)/shard_map/dot_general | solution.py:38
  558.3 32.7 %all-to-all-done.5 = bf16[2,8,128,512]{3,1,0,2:T(8,128)(2,1)S(1)} async-done(((bf16[2,8,128,512]{3,1,0,2:T(8,128)(2,1)}), bf16[2,8,128,512]{3,1,0,2:T(8,128)(2,1)S(1)}, u32[]{:S(2)}, u32[]{:S(2)}) %all-to-all-start.5) | async-done | bytes 2097184 | tf_op jit(solution)/shard_map/all_to_all | solution.py:73
  591.0 7.0 all-to-all-start.3
  598.0 14.7 %fusion.26 = f32[2048,1024]{0,1:T(8,128)} fusion(bf16[2048,2048]{1,0:T(8,128)(2,1)} %get-tuple-element.4, bf16[2048,1024]{1,0:T(8,128)(2,1)} %all-gather.11.cloned.1.call-done), kind=kOutput, calls=%fused_computation.41 | convolution fusion | flops 8589934592 | bytes 20971520 | tf_op jit(solution)/shard_map/dot_general | solution.py:53
  616.5 5.5 copy.97
  622.0 6.3 fusion.4
  628.3 6.4 copy.103
  634.7 55.5 %all-to-all-done.3 = f32[2048,2,512]{0,2,1:T(8,128)} async-done(((f32[2048,2,512]{0,2,1:T(8,128)}), f32[2048,2,512]{0,2,1:T(8,128)}, u32[]{:S(2)}, u32[]{:S(2)}) %all-to-all-start.3) | async-done | bytes 8388640 | tf_op jit(solution)/shard_map/all_to_all | solution.py:39
  690.2 5.9 all-to-all-start.7
  696.1 6.5 convert_bitcast_fusion.3
  702.6 6.4 copy.98
  708.9 51.4 %all-to-all-done.7 = bf16[2,128,8,512]{3,0,2,1:T(2,128)(2,1)} async-done(((bf16[2,128,8,512]{3,0,2,1:T(2,128)(2,1)}), bf16[2,128,8,512]{3,0,2,1:T(2,128)(2,1)}, u32[]{:S(2)}, u32[]{:S(2)}) %all-to-all-start.7) | async-done | bytes 2097184 | tf_op jit(solution)/shard_map/all_to_all | solution.py:80
  767.9 6.6 reduce_sum.22
  774.5 5.3 copy.112
  779.8 5.5 fusion.7
  787.3 25.5 %all-to-all-done.6 = bf16[2,128,8,512]{3,0,2,1:T(2,128)(2,1)} async-done(((bf16[2,128,8,512]{3,0,2,1:T(2,128)(2,1)}), bf16[2,128,8,512]{3,0,2,1:T(2,128)(2,1)}, u32[]{:S(2)}, u32[]{:S(2)}) %all-to-all-start.6) | async-done | bytes 2097184 | tf_op jit(solution)/shard_map/all_to_all | solution.py:86
  (70 shorter events, 70.9 us)
Async XLA Ops:
  7.2 137.1 %copy-start = (bf16[8,128,128]{2,1,0:T(8,128)(2,1)S(1)}, bf16[8,128,128]{2,1,0:T(8,128)(2,1)}, u32[]{:S(2)}) copy-start(bf16[8,128,128]{2,1,0:T(8,128)(2,1)} %param.10) | copy-start | bytes 786436
  7.2 10.7 %copy-start.7 = (bf16[8,128,128]{2,1,0:T(8,128)(2,1)S(1)}, bf16[8,128,128]{2,1,0:T(8,128)(2,1)}, u32[]{:S(2)}) copy-start(bf16[8,128,128]{2,1,0:T(8,128)(2,1)} %param.9) | copy-start | bytes 786436
  11.4 54.0 %all-to-all-start = ((bf16[2,8,128,512]{3,1,0,2:T(8,128)(2,1)}), bf16[2,8,128,512]{3,1,0,2:T(8,128)(2,1)S(1)}, u32[]{:S(2)}, u32[]{:S(2)}) async-start(bf16[2,8,128,512]{3,1,0,2:T(8,128)(2,1)} %copy.79), calls=%async_computation | async-start | bytes 4194304 | tf_op jit(solution)/shard_map/all_to_all | solution.py:23
  65.3 75.9 %all-to-all-start.1 = ((bf16[2,8,128,512]{3,0,1,2:T(2,128)(2,1)}), bf16[2,8,128,512]{3,0,1,2:T(2,128)(2,1)}, u32[]{:S(2)}, u32[]{:S(2)}) async-start(bf16[2,8,128,512]{3,0,1,2:T(2,128)(2,1)} %copy.84), calls=%async_computation.1 | async-start | bytes 4194304 | tf_op jit(solution)/shard_map/all_to_all | solution.py:22
  70.2 141.2 %all-gather.7.cloned.1.call-start = ((), (), s32[]{:S(2)}) async-start(), calls=%async_computation.11 | async-start | bytes 4456448 | tf_op jit(solution)/shard_map/all_gather | solution.py:33
  71.0 195.4 %all-gather.5.cloned.1.call-start = ((), (), s32[]{:S(2)}) async-start(), calls=%async_computation.10 | async-start | bytes 6291456 | tf_op jit(solution)/shard_map/all_gather | solution.py:35
  143.9 2.9 copy-start.1
  144.0 2.9 copy-start.9
  144.0 2.9 copy-start.11
  145.5 1.3 copy-start.4
  207.0 1.3 copy-start.2
  209.9 114.8 %all-gather.11.cloned.1.call-start = ((), (), s32[]{:S(2)}) async-start(), calls=%async_computation.13 | async-start | bytes 6291456 | tf_op jit(solution)/shard_map/all_gather | solution.py:47
  210.6 166.2 %all-gather.9.cloned.1.call-start = ((), (), s32[]{:S(2)}) async-start(), calls=%async_computation.12 | async-start | bytes 4456448 | tf_op jit(solution)/shard_map/all_gather | solution.py:34
  211.2 605.8 %reduce-scatter.3.cloned.1.call-start = ((), (), s32[]{:S(2)}) async-start(), calls=%async_computation.14 | async-start | bytes 8912896 | tf_op jit(solution)/shard_map/reduce_scatter | solution.py:62
  376.9 22.4 %copy-start.13 = (bf16[2048,1024]{1,0:T(8,128)(2,1)S(1)}, bf16[2048,1024]{1,0:T(8,128)(2,1)}, u32[]{:S(2)}) copy-start(bf16[2048,1024]{1,0:T(8,128)(2,1)} %all-gather.5.cloned.1.call-done) | copy-start | bytes 12582916
  396.1 3.3 copy-start.14
  526.5 5.5 copy-start.6
  537.5 53.5 %all-to-all-start.5 = ((bf16[2,8,128,512]{3,1,0,2:T(8,128)(2,1)}), bf16[2,8,128,512]{3,1,0,2:T(8,128)(2,1)S(1)}, u32[]{:S(2)}, u32[]{:S(2)}) async-start(bf16[2,8,128,512]{3,1,0,2:T(8,128)(2,1)} %copy.94), calls=%async_computation.5 | async-start | bytes 4194304 | tf_op jit(solution)/shard_map/all_to_all | solution.py:73
  591.0 99.2 %all-to-all-start.3 = ((f32[2048,2,512]{0,2,1:T(8,128)}), f32[2048,2,512]{0,2,1:T(8,128)}, u32[]{:S(2)}, u32[]{:S(2)}) async-start(f32[2048,2,512]{0,2,1:T(8,128)} %bitcast.95), calls=%async_computation.3 | async-start | bytes 16777216 | tf_op jit(solution)/shard_map/all_to_all | solution.py:39
  597.9 221.0 %reduce-scatter.5.cloned.1.call-start = ((), (), s32[]{:S(2)}) async-start(), calls=%async_computation.15 | async-start | bytes 8912896 | tf_op jit(solution)/shard_map/reduce_scatter | solution.py:56
  616.5 5.5 copy-start.5
  616.5 5.5 copy-start.10
  616.5 5.5 copy-start.12
  690.2 70.1 %all-to-all-start.7 = ((bf16[2,128,8,512]{3,0,2,1:T(2,128)(2,1)}), bf16[2,128,8,512]{3,0,2,1:T(2,128)(2,1)}, u32[]{:S(2)}, u32[]{:S(2)}) async-start(bf16[2,128,8,512]{3,0,2,1:T(2,128)(2,1)} %copy.103), calls=%async_computation.7 | async-start | bytes 4194304 | tf_op jit(solution)/shard_map/all_to_all | solution.py:80
  702.6 62.7 %copy-start.3 = (bf16[2,128,8,512]{3,2,1,0:T(8,128)(2,1)S(1)}, bf16[2,128,8,512]{3,2,1,0:T(8,128)(2,1)}, u32[]{:S(2)}) copy-start(bf16[2,128,8,512]{3,2,1,0:T(8,128)(2,1)} %copy-done.2) | copy-start | bytes 6291460
  760.3 52.5 %all-to-all-start.6 = ((bf16[2,128,8,512]{3,0,2,1:T(2,128)(2,1)}), bf16[2,128,8,512]{3,0,2,1:T(2,128)(2,1)}, u32[]{:S(2)}, u32[]{:S(2)}) async-start(bf16[2,128,8,512]{3,0,2,1:T(2,128)(2,1)} %copy.98), calls=%async_computation.6 | async-start | bytes 4194304 | tf_op jit(solution)/shard_map/all_to_all | solution.py:86
  785.3 29.4 %copy-start.8 = (bf16[8,128,128]{2,1,0:T(8,128)(2,1)S(1)}, bf16[8,128,128]{2,1,0:T(8,128)(2,1)}, u32[]{:S(2)}) copy-start(bf16[8,128,128]{2,1,0:T(8,128)(2,1)} %param.9) | copy-start | bytes 786436
Sparse Core Ops, SparseCore 0:
  73.2 71.5 all-gather.6
  210.0 56.3 all-gather.4
  267.9 56.7 all-gather.10
  326.7 50.0 all-gather.8
  410.9 103.7 reduce-scatter.2
  612.8 132.9 reduce-scatter.4
where the time goes:
time: 837 us; the launch traced here: 828 us
  waiting for transfers between devices  412 us (49%)
  blocking collectives  149 us (18%)
  matrix products  103 us (12%)
  local copies, waits for them, and re-layouts  76.3 us (9%)
  other arithmetic  36.9 us (4%)
  starting transfers between devices  35.8 us (4%)
  between operations  14.5 us (2%)
    all_to_all x1, blocking collectives, body(): lax.all_to_all(back_term, 'fsdp', split_axis=1, concat_axis=0, tiled=True)  96.6 us
    all_to_all x1, waiting for transfers between devices, body(): lax.all_to_all(section_one, 'seq', split_axis=2, concat_axis=1, tiled=True)  61 us
    all_to_all x1, waiting for transfers between devices, body(): lax.all_to_all(partial_out, 'fsdp', split_axis=1, concat_axis=0, tiled=True)  55.5 us
    all_gather x1, waiting for transfers between devices, body(): mixed_all = lax.all_gather(mixed, 'fsdp', axis=1, tiled=True)  54.9 us
    all_gather x1, waiting for transfers between devices, body(): full_out = lax.all_gather(out_weight, 'seq', axis=1, tiled=True)  52.1 us
    all_to_all x1, blocking collectives, body(): lax.all_to_all(gated_cols, 'seq', split_axis=1, concat_axis=2, tiled=True)  52.1 us
    all_to_all x1, waiting for transfers between devices, body(): lax.all_to_all(gate_term.astype(jnp.bfloat16), 'seq', split_axis=1, conca...  51.4 us
    all_gather x1, waiting for transfers between devices, body(): upstream_all = lax.all_gather(upstream, 'fsdp', axis=1, tiled=True)  39.7 us
  transfers between devices with their start and end apart: 12, of which 9 were waited for; matrix products, arithmetic and copies ran while one was open for 21% of the time, Pallas kernels for 0%

commit v1 on v0

--- a/solution.py
+++ b/solution.py
@@ -31,7 +31,14 @@
     mixed_grid = lax.all_to_all(gated_cols, "seq", split_axis=1, concat_axis=2, tiled=True)
     mixed = mixed_grid.reshape(row_count, chan_count)
     full_in = lax.all_gather(in_weight, "seq", axis=0, tiled=True)
-    full_out = lax.all_gather(out_weight, "seq", axis=1, tiled=True)
+    ways, here = (lax.axis_size("seq"), lax.axis_index("seq"))
+    full_out, reach = (out_weight, 1)
+    while reach < ways:
+        theirs = lax.ppermute(full_out, "seq", [(d, d ^ reach) for d in range(ways)])
+        mine_first = jnp.concatenate([full_out, theirs], axis=1)
+        theirs_first = jnp.concatenate([theirs, full_out], axis=1)
+        full_out = jnp.where(here & reach == 0, mine_first, theirs_first)
+        reach = 2 * reach
     mixed_all = lax.all_gather(mixed, "fsdp", axis=1, tiled=True)
     pre_act = jnp.dot(mixed_all, full_in, preferred_element_type=jnp.float32)
     hidden = jax.nn.silu(pre_act).astype(jnp.bfloat16)

time: 837 us -> 808 us (0.965)
  waiting for transfers between devices: 412 us -> 371 us
    ppermute x0 -> x4, waiting for transfers between devices: none -> 95.6 us  [body(): lax.ppermute(full_out, 'seq', [(d, d ^ reach) for d in range(ways)])]
    all_gather x1 -> x0, waiting for transfers between devices: 52.1 us -> none  [body(): full_out = lax.all_gather(out_weight, 'seq', axis=1, tiled=True)]
    all_gather x1, waiting for transfers between devices: 54.9 us -> 13.2 us  [body(): mixed_all = lax.all_gather(mixed, 'fsdp', axis=1, tiled=True)]
    all_gather x1, waiting for transfers between devices: 39.7 us -> 0.01 us  [body(): upstream_all = lax.all_gather(upstream, 'fsdp', axis=1, tiled=True)]
  transfers between devices with their start and end apart: 12 -> 15, of which waited for: 9 -> 11; matrix products, arithmetic and copies ran while one was open for 21% -> 22% of each run, Pallas kernels for 0% -> 0%
where the time goes in v1:
time: 808 us; the launch traced here: 798 us
  waiting for transfers between devices  371 us (46%)
  blocking collectives  148 us (18%)
  matrix products  111 us (14%)
  local copies, waits for them, and re-layouts  73 us (9%)
  starting transfers between devices  41.1 us (5%)
  other arithmetic  39.7 us (5%)
  between operations  14.3 us (2%)
    all_to_all x1, blocking collectives, body(): lax.all_to_all(back_term, 'fsdp', split_axis=1, concat_axis=0, tiled=True)  96.1 us
    ppermute x4, waiting for transfers between devices, body(): lax.ppermute(full_out, 'seq', [(d, d ^ reach) for d in range(ways)])  95.6 us
    all_to_all x1, waiting for transfers between devices, body(): lax.all_to_all(section_one, 'seq', split_axis=2, concat_axis=1, tiled=True)  61 us
    all_to_all x1, waiting for transfers between devices, body(): lax.all_to_all(partial_out, 'fsdp', split_axis=1, concat_axis=0, tiled=True)  55.6 us
    all_to_all x1, blocking collectives, body(): lax.all_to_all(gated_cols, 'seq', split_axis=1, concat_axis=2, tiled=True)  52 us
    all_to_all x1, waiting for transfers between devices, body(): lax.all_to_all(gate_term.astype(jnp.bfloat16), 'seq', split_axis=1, conca...  51.4 us
    all_to_all x1, waiting for transfers between devices, body(): lax.all_to_all(source, 'seq', split_axis=2, concat_axis=1, tiled=True)  37.5 us
    all_to_all x1, waiting for transfers between devices, body(): lax.all_to_all(mixed_grad, 'seq', split_axis=2, concat_axis=1, tiled=True)  30.3 us
  transfers between devices with their start and end apart: 15, of which 11 were waited for; matrix products, arithmetic and copies ran while one was open for 22% of the time, Pallas kernels for 0%

profile of v1, /device:TPU:11, one launch (start us, length us, event | category | flops | bytes accessed | tf_op | source)
XLA Modules:
  0.0 798.2 jit_solution(16469230142204980038)
XLA Ops:
  11.3 6.6 all-to-all-start
  21.6 6.2 copy.88
  27.8 37.5 %all-to-all-done = bf16[2,8,128,512]{3,1,0,2:T(8,128)(2,1)S(1)} async-done(((bf16[2,8,128,512]{3,1,0,2:T(8,128)(2,1)}), bf16[2,8,128,512]{3,1,0,2:T(8,128)(2,1)S(1)}, u32[]{:S(2)}, u32[]{:S(2)}) %all-to-all-start) | async-done | bytes 2097184 | tf_op jit(solution)/shard_map/all_to_all | solution.py:23
  80.2 61.0 %all-to-all-done.1 = bf16[2,8,128,512]{3,0,1,2:T(2,128)(2,1)} async-done(((bf16[2,8,128,512]{3,0,1,2:T(2,128)(2,1)}), bf16[2,8,128,512]{3,0,1,2:T(2,128)(2,1)}, u32[]{:S(2)}, u32[]{:S(2)}) %all-to-all-start.1) | async-done | bytes 2097184 | tf_op jit(solution)/shard_map/all_to_all | solution.py:22
  154.7 52.0 %all_to_all.104 = bf16[2,128,8,512]{3,0,2,1:T(2,128)(2,1)S(1)} all-to-all(bf16[2,128,8,512]{3,0,2,1:T(2,128)(2,1)S(1)} %copy.92), channel_id=1, replica_groups=mesh['seq'=16,'fsdp'=2] {'seq'}, dimensions={1} | all-to-all | bytes 4194304 | tf_op jit(solution)/shard_map/all_to_all | solution.py:31
  212.6 12.6 %collective-permute-done.1 = bf16[2048,128]{0,1:T(8,128)(2,1)S(1)} collective-permute-done((bf16[2048,128]{0,1:T(8,128)(2,1)S(1)}, bf16[2048,128]{0,1:T(8,128)(2,1)S(1)}, u32[]{:S(2)}, u32[]{:S(2)}) %collective-permute-start.1) | collective-permute-done | bytes 524320 | tf_op jit(solution)/shard_map/ppermute | solution.py:37
  225.9 23.5 %collective-permute-done.2 = bf16[2048,256]{0,1:T(8,128)(2,1)} collective-permute-done((bf16[2048,256]{0,1:T(8,128)(2,1)S(1)}, bf16[2048,256]{0,1:T(8,128)(2,1)}, u32[]{:S(2)}, u32[]{:S(2)}) %collective-permute-start.2) | collective-permute-done | bytes 1048608 | tf_op jit(solution)/shard_map/ppermute | solution.py:37
  253.3 13.2 %all-gather.4.cloned.1.call-done = bf16[2048,1024]{1,0:T(8,128)(2,1)} async-done(((bf16[2048,512]{1,0:T(8,128)(2,1)}), bf16[2048,1024]{1,0:T(8,128)(2,1)}) %all-gather.4.cloned.1.call-update) | async-done | bytes 4194320 | tf_op jit(solution)/shard_map/all_gather | solution.py:42
  266.4 18.8 %multiply_convert_fusion = (bf16[2048,2048]{1,0:T(8,128)(2,1)}, f32[2048,2048]{1,0:T(8,128)}) fusion(bf16[2048,1024]{1,0:T(8,128)(2,1)} %all-gather.4.cloned.1.call-done, bf16[1024,2048]{1,0:T(8,128)(2,1)} %all-gather.6.cloned.1.call-done), kind=kOutput, calls=%fused_computation.3 | convolution fusion | flops 8610906112 | bytes 33554432 | tf_op jit(solution)/shard_map/dot_general | solution.py:43
  285.2 58.2 %collective-permute-done.3 = bf16[2048,512]{0,1:T(8,128)(2,1)} collective-permute-done((bf16[2048,512]{0,1:T(8,128)(2,1)S(1)}, bf16[2048,512]{0,1:T(8,128)(2,1)}, u32[]{:S(2)}, u32[]{:S(2)}) %collective-permute-start.3) | collective-permute-done | bytes 2097184 | tf_op jit(solution)/shard_map/ppermute | solution.py:37
  343.4 21.0 %fusion.1 = bf16[2048,2048]{1,0:T(8,128)(2,1)} fusion(f32[2048,2048]{1,0:T(8,128)} %get-tuple-element.5, bf16[2048,1024]{1,0:T(8,128)(2,1)} %all-gather.8.cloned.1.call-done, bf16[2048,512]{0,1:T(8,128)(2,1)} %collective-permute-done.3, bf16[2048,512]{0,1:T(8,128)(2,1)S(1)} %maximum_select_fusion.1, pred[]{:T(512)S(6)} %eq.12), kind=kOutput, calls=%fused_computation.2 | convolution fusion | flops 8646557696 | bytes 33554432 | tf_op jit(solution)/shard_map/dot_general | solution.py:55
  364.4 15.0 %fusion.29 = f32[1024,2048]{1,0:T(8,128)} fusion(bf16[2048,1024]{1,0:T(8,128)(2,1)} %all-gather.4.cloned.1.call-done, bf16[2048,2048]{1,0:T(8,128)(2,1)} %fusion.1), kind=kOutput, calls=%fused_computation.48 | convolution fusion | flops 8589934592 | bytes 20971520 | tf_op jit(solution)/shard_map/dot_general | solution.py:66
  379.4 12.6 %fusion.28 = f32[2048,1024]{0,1:T(8,128)S(1)} fusion(bf16[2048,2048]{1,0:T(8,128)(2,1)} %fusion.1, bf16[1024,2048]{1,0:T(8,128)(2,1)} %all-gather.6.cloned.1.call-done), kind=kOutput, calls=%fused_computation.47 | convolution fusion | flops 8589934592 | bytes 20971520 | tf_op jit(solution)/shard_map/dot_general | solution.py:70
  392.0 96.1 %all_to_all.105 = f32[2048,2,512]{0,2,1:T(8,128)} all-to-all(f32[2048,2,512]{0,2,1:T(8,128)S(1)} %bitcast.100), channel_id=1, replica_groups=mesh['seq'=16,'fsdp'=2] {'fsdp'}, dimensions={1} | all-to-all | bytes 16777216 | tf_op jit(solution)/shard_map/all_to_all | solution.py:73
  488.2 6.6 reduce_sum.24
  494.8 5.5 copy.119
  505.7 8.5 %all-to-all-start.5 = ((bf16[2,8,128,512]{3,1,0,2:T(8,128)(2,1)}), bf16[2,8,128,512]{3,1,0,2:T(8,128)(2,1)S(1)}, u32[]{:S(2)}, u32[]{:S(2)}) async-start(bf16[2,8,128,512]{3,1,0,2:T(8,128)(2,1)} %copy.99), calls=%async_computation.5 | async-start | bytes 4194304 | tf_op jit(solution)/shard_map/all_to_all | solution.py:80
  514.3 17.0 %fusion.21 = f32[2048,1024]{0,1:T(8,128)} fusion(bf16[2048,2048]{1,0:T(8,128)(2,1)} %get-tuple-element.4, bf16[2048,512]{0,1:T(8,128)(2,1)} %collective-permute-done.3, bf16[2048,512]{0,1:T(8,128)(2,1)} %copy-done.7, pred[]{:T(512)S(6)} %eq.12), kind=kOutput, calls=%fused_computation.37 | convolution fusion | flops 8608808960 | bytes 20971520 | tf_op jit(solution)/shard_map/dot_general | solution.py:45
  531.3 30.3 %all-to-all-done.5 = bf16[2,8,128,512]{3,1,0,2:T(8,128)(2,1)S(1)} async-done(((bf16[2,8,128,512]{3,1,0,2:T(8,128)(2,1)}), bf16[2,8,128,512]{3,1,0,2:T(8,128)(2,1)S(1)}, u32[]{:S(2)}, u32[]{:S(2)}) %all-to-all-start.5) | async-done | bytes 2097184 | tf_op jit(solution)/shard_map/all_to_all | solution.py:80
  561.6 7.0 all-to-all-start.3
  568.6 14.6 %fusion.30 = f32[2048,1024]{0,1:T(8,128)} fusion(bf16[2048,2048]{1,0:T(8,128)(2,1)} %get-tuple-element.4, bf16[2048,1024]{1,0:T(8,128)(2,1)} %all-gather.8.cloned.1.call-done), kind=kOutput, calls=%fused_computation.49 | convolution fusion | flops 8589934592 | bytes 20971520 | tf_op jit(solution)/shard_map/dot_general | solution.py:60
  587.1 5.5 copy.102
  592.6 6.3 fusion.6
  598.9 6.3 copy.108
  605.2 55.6 %all-to-all-done.3 = f32[2048,2,512]{0,2,1:T(8,128)} async-done(((f32[2048,2,512]{0,2,1:T(8,128)}), f32[2048,2,512]{0,2,1:T(8,128)}, u32[]{:S(2)}, u32[]{:S(2)}) %all-to-all-start.3) | async-done | bytes 8388640 | tf_op jit(solution)/shard_map/all_to_all | solution.py:46
  660.8 5.7 all-to-all-start.7
  666.6 6.5 convert_bitcast_fusion.3
  673.1 6.4 copy.103
  679.5 51.4 %all-to-all-done.7 = bf16[2,128,8,512]{3,0,2,1:T(2,128)(2,1)} async-done(((bf16[2,128,8,512]{3,0,2,1:T(2,128)(2,1)}), bf16[2,128,8,512]{3,0,2,1:T(2,128)(2,1)}, u32[]{:S(2)}, u32[]{:S(2)}) %all-to-all-start.7) | async-done | bytes 2097184 | tf_op jit(solution)/shard_map/all_to_all | solution.py:87
  738.7 6.6 reduce_sum.22
  750.7 5.5 fusion.9
  758.2 25.3 %all-to-all-done.6 = bf16[2,128,8,512]{3,0,2,1:T(2,128)(2,1)} async-done(((bf16[2,128,8,512]{3,0,2,1:T(2,128)(2,1)}), bf16[2,128,8,512]{3,0,2,1:T(2,128)(2,1)}, u32[]{:S(2)}, u32[]{:S(2)}) %all-to-all-start.6) | async-done | bytes 2097184 | tf_op jit(solution)/shard_map/all_to_all | solution.py:93
  (78 shorter events, 79.0 us)
Async XLA Ops:
  7.2 137.0 %copy-start = (bf16[8,128,128]{2,1,0:T(8,128)(2,1)S(1)}, bf16[8,128,128]{2,1,0:T(8,128)(2,1)}, u32[]{:S(2)}) copy-start(bf16[8,128,128]{2,1,0:T(8,128)(2,1)} %param.10) | copy-start | bytes 786436
  7.2 10.7 %copy-start.8 = (bf16[8,128,128]{2,1,0:T(8,128)(2,1)S(1)}, bf16[8,128,128]{2,1,0:T(8,128)(2,1)}, u32[]{:S(2)}) copy-start(bf16[8,128,128]{2,1,0:T(8,128)(2,1)} %param.9) | copy-start | bytes 786436
  11.3 54.0 %all-to-all-start = ((bf16[2,8,128,512]{3,1,0,2:T(8,128)(2,1)}), bf16[2,8,128,512]{3,1,0,2:T(8,128)(2,1)S(1)}, u32[]{:S(2)}, u32[]{:S(2)}) async-start(bf16[2,8,128,512]{3,1,0,2:T(8,128)(2,1)} %copy.83), calls=%async_computation | async-start | bytes 4194304 | tf_op jit(solution)/shard_map/all_to_all | solution.py:23
  65.3 75.9 %all-to-all-start.1 = ((bf16[2,8,128,512]{3,0,1,2:T(2,128)(2,1)}), bf16[2,8,128,512]{3,0,1,2:T(2,128)(2,1)}, u32[]{:S(2)}, u32[]{:S(2)}) async-start(bf16[2,8,128,512]{3,0,1,2:T(2,128)(2,1)} %copy.88), calls=%async_computation.1 | async-start | bytes 4194304 | tf_op jit(solution)/shard_map/all_to_all | solution.py:22
  70.2 183.0 %all-gather.6.cloned.1.call-start = ((), (), s32[]{:S(2)}) async-start(), calls=%async_computation.11 | async-start | bytes 4456448 | tf_op jit(solution)/shard_map/all_gather | solution.py:33
  71.0 195.5 %all-gather.4.cloned.1.call-start = ((), (), s32[]{:S(2)}) async-start(), calls=%async_computation.10 | async-start | bytes 6291456 | tf_op jit(solution)/shard_map/all_gather | solution.py:42
  143.9 2.9 copy-start.1
  144.0 2.9 copy-start.11
  144.0 2.9 copy-start.13
  145.5 1.3 copy-start.4
  207.0 1.3 copy-start.2
  207.1 2.9 copy-start.10
  209.9 133.5 %all-gather.8.cloned.1.call-start = ((), (), s32[]{:S(2)}) async-start(), calls=%async_computation.12 | async-start | bytes 6291456 | tf_op jit(solution)/shard_map/all_gather | solution.py:54
  210.0 1.6 collective-permute-start
  211.7 13.5 %collective-permute-start.1 = (bf16[2048,128]{0,1:T(8,128)(2,1)S(1)}, bf16[2048,128]{0,1:T(8,128)(2,1)S(1)}, u32[]{:S(2)}, u32[]{:S(2)}) collective-permute-start(bf16[2048,128]{0,1:T(8,128)(2,1)S(1)} %maximum_select_fusion.5), channel_id=1, source_target_pairs={{0,4},{2,6},{4,0},{6,2},{8,12},{10,14},{12,8},{14,10},{16,20},{18,... | collective-permute-start | bytes 1572872 | tf_op jit(solution)/shard_map/ppermute | solution.py:37
  225.4 23.9 %collective-permute-start.2 = (bf16[2048,256]{0,1:T(8,128)(2,1)S(1)}, bf16[2048,256]{0,1:T(8,128)(2,1)}, u32[]{:S(2)}, u32[]{:S(2)}) collective-permute-start(bf16[2048,256]{0,1:T(8,128)(2,1)S(1)} %maximum_select_fusion.2), channel_id=1, source_target_pairs={{0,8},{2,10},{4,12},{6,14},{8,0},{10,2},{12,4},{14,6},{16,24},{18,... | collective-permute-start | bytes 3145736 | tf_op jit(solution)/shard_map/ppermute | solution.py:37
  225.8 561.8 %reduce-scatter.3.cloned.1.call-start = ((), (), s32[]{:S(2)}) async-start(), calls=%async_computation.13 | async-start | bytes 8912896 | tf_op jit(solution)/shard_map/reduce_scatter | solution.py:69
  251.8 91.6 %copy-start.7 = (bf16[2048,512]{0,1:T(8,128)(2,1)}, bf16[2048,512]{0,1:T(8,128)(2,1)S(1)}, u32[]{:S(2)}) copy-start(bf16[2048,512]{0,1:T(8,128)(2,1)S(1)} %maximum_select_fusion.1) | copy-start | bytes 6291460
  251.9 91.6 %collective-permute-start.3 = (bf16[2048,512]{0,1:T(8,128)(2,1)S(1)}, bf16[2048,512]{0,1:T(8,128)(2,1)}, u32[]{:S(2)}, u32[]{:S(2)}) collective-permute-start(bf16[2048,512]{0,1:T(8,128)(2,1)S(1)} %maximum_select_fusion.1), channel_id=1, source_target_pairs={{0,16},{2,18},{4,20},{6,22},{8,24},{10,26},{12,28},{14,30},{16,0},... | collective-permute-start | bytes 6291464 | tf_op jit(solution)/shard_map/ppermute | solution.py:37
  494.8 5.5 copy-start.6
  505.7 55.8 %all-to-all-start.5 = ((bf16[2,8,128,512]{3,1,0,2:T(8,128)(2,1)}), bf16[2,8,128,512]{3,1,0,2:T(8,128)(2,1)S(1)}, u32[]{:S(2)}, u32[]{:S(2)}) async-start(bf16[2,8,128,512]{3,1,0,2:T(8,128)(2,1)} %copy.99), calls=%async_computation.5 | async-start | bytes 4194304 | tf_op jit(solution)/shard_map/all_to_all | solution.py:80
  561.6 99.3 %all-to-all-start.3 = ((f32[2048,2,512]{0,2,1:T(8,128)}), f32[2048,2,512]{0,2,1:T(8,128)}, u32[]{:S(2)}, u32[]{:S(2)}) async-start(f32[2048,2,512]{0,2,1:T(8,128)} %bitcast.99), calls=%async_computation.3 | async-start | bytes 16777216 | tf_op jit(solution)/shard_map/all_to_all | solution.py:46
  568.6 221.0 %reduce-scatter.5.cloned.1.call-start = ((), (), s32[]{:S(2)}) async-start(), calls=%async_computation.14 | async-start | bytes 8912896 | tf_op jit(solution)/shard_map/reduce_scatter | solution.py:63
  587.1 5.5 copy-start.5
  587.1 5.5 copy-start.12
  587.1 5.5 copy-start.14
  660.8 70.0 %all-to-all-start.7 = ((bf16[2,128,8,512]{3,0,2,1:T(2,128)(2,1)}), bf16[2,128,8,512]{3,0,2,1:T(2,128)(2,1)}, u32[]{:S(2)}, u32[]{:S(2)}) async-start(bf16[2,128,8,512]{3,0,2,1:T(2,128)(2,1)} %copy.108), calls=%async_computation.7 | async-start | bytes 4194304 | tf_op jit(solution)/shard_map/all_to_all | solution.py:87
  673.1 63.1 %copy-start.3 = (bf16[2,128,8,512]{3,2,1,0:T(8,128)(2,1)S(1)}, bf16[2,128,8,512]{3,2,1,0:T(8,128)(2,1)}, u32[]{:S(2)}) copy-start(bf16[2,128,8,512]{3,2,1,0:T(8,128)(2,1)} %copy-done.2) | copy-start | bytes 6291460
  730.8 52.6 %all-to-all-start.6 = ((bf16[2,128,8,512]{3,0,2,1:T(2,128)(2,1)}), bf16[2,128,8,512]{3,0,2,1:T(2,128)(2,1)}, u32[]{:S(2)}, u32[]{:S(2)}) async-start(bf16[2,128,8,512]{3,0,2,1:T(2,128)(2,1)} %copy.103), calls=%async_computation.6 | async-start | bytes 4194304 | tf_op jit(solution)/shard_map/all_to_all | solution.py:93
  756.2 29.2 %copy-start.9 = (bf16[8,128,128]{2,1,0:T(8,128)(2,1)S(1)}, bf16[8,128,128]{2,1,0:T(8,128)(2,1)}, u32[]{:S(2)}) copy-start(bf16[8,128,128]{2,1,0:T(8,128)(2,1)} %param.9) | copy-start | bytes 786436
Sparse Core Ops, SparseCore 0:
  73.2 71.5 all-gather.5
  210.0 56.3 all-gather.3
  268.0 56.7 all-gather.7
  379.6 106.5 reduce-scatter.2
  583.3 132.8 reduce-scatter.4
